TPU v7x, 128 devices: a whole 4x4x4 slice. The times are simulated.
128 devices in a mesh: dp: 4 (over z), latent: 32 (over x, y, core).
Axes of the slice: x: 4, y: 4, z: 4, core: 2. Of those that a mesh axis runs over, the one named last changes fastest.
Arguments:
- acts: bfloat16 [640, 8192], P(('dp', 'latent')), may hold values from -6 to 6
- chat_len: int32 [128], P(('dp', 'latent')), may hold values from 1 to 5, as said below
- group_of: int32 [640, 1], P(('dp', 'latent')), may hold values from 0 to 4; in each aligned block of 5 rows (0 to 4, 5 to 9, ...) no two rows name the same one
- w_enc: bfloat16 [2, 4096, 16384], P(None, None, 'latent'), may hold values from -0.0625 to 0.0625
- b_enc: float32 [16384], P('latent'), may hold values from -3 to 3
- w_dec: bfloat16 [16384, 8192], P('latent'), may hold values from -0.046875 to 0.046875
- b_dec: float32 [2, 4096], replicated, may hold values from -3 to 3
Outputs:
- grad_enc: bfloat16 [2, 4096, 16384], P(None, 'dp', 'latent')
- grad_dec: bfloat16 [16384, 8192], P('latent', 'dp')
- loss: float32 [], replicated
Inputs may be any that keep to these rules, and one draw needn't show every extreme that they name: `chat_len`: the last serving shard harvests all 5 rows. `group_of`: among the 5 row slots of each serving shard every value 0 to 4 appears exactly once.
All inputs are finite; a program needn't handle non-finite values.
Results may differ from a plain program's by a relative error of at most 0.02.
Values may be sent and summed in bfloat16 or wider, within the bound.
No kernel may reach another device: no remote copies, remote signals or barrier semaphores. Data moves between devices by JAX's collectives and lax.ppermute only.
A program may use at most 128 MiB of HBM per device.

v0:
```python
import jax
import jax.numpy as jnp
from jax import lax
from jax.sharding import PartitionSpec as P

sparsity_weight = 1.0
loss_scale = 8.0
norm_eps = 1e-06


def shards(acts, chat_len, group_of, w_enc, b_enc, w_dec, b_dec):
    groups = lax.axis_size("dp")
    slots = acts.shape[0]
    width = acts.shape[1]
    half = width // 2
    local_latents = w_enc.shape[2]
    capacity = slots // (groups + 1)
    slot_ids = jnp.arange(slots, dtype=jnp.int32)
    alive = (slot_ids < chat_len[0]).astype(jnp.float32)
    order = jnp.argsort(group_of[:, 0], stable=True)[: groups * capacity]
    own_count = jnp.sum(alive[order])
    outgoing = acts[order].reshape(groups, capacity, width)
    out_mask = alive[order].reshape(groups, capacity).astype(jnp.bfloat16)
    received, recv_mask = (
        lax.all_to_all(outgoing, "dp", split_axis=0, concat_axis=0, tiled=True),
        lax.all_to_all(out_mask, "dp", split_axis=0, concat_axis=0, tiled=True),
    )
    member_rows, member_mask = (
        lax.all_gather(received, "latent", axis=0, tiled=True),
        lax.all_gather(recv_mask, "latent", axis=0, tiled=True),
    )
    xg = member_rows.reshape(-1, width)
    maskg = member_mask.reshape(-1).astype(jnp.float32)
    total_rows = xg.shape[0]
    share_rows = total_rows // lax.axis_size("latent")
    first_row = lax.axis_index("latent") * share_rows
    wenc_flat = w_enc.reshape(width, local_latents)
    squares_dec = jnp.square(w_dec.astype(jnp.float32))
    norm_base = jnp.sqrt(jnp.sum(squares_dec[:, :half], axis=1) + norm_eps)
    norm_inst = jnp.sqrt(jnp.sum(squares_dec[:, half:], axis=1) + norm_eps)
    norm_sum = norm_base + norm_inst
    column_ids = jnp.arange(width, dtype=jnp.int32)
    bias_row = b_dec.reshape(width)
    pre = jnp.dot(xg, wenc_flat, preferred_element_type=jnp.float32) + b_enc[None, :]
    act = jnp.maximum(pre, 0.0)
    feats = act * act
    feats16 = feats.astype(jnp.bfloat16)
    partial_value = jnp.dot(feats16, w_dec, preferred_element_type=jnp.float32)
    recon = lax.psum(partial_value.astype(jnp.bfloat16), "latent").astype(jnp.float32)
    err = (recon + bias_row[None, :] - xg.astype(jnp.float32)) * maskg[:, None]
    err16 = err.astype(jnp.bfloat16)
    err_share = lax.dynamic_slice_in_dim(err, first_row, share_rows, 0)
    square_sum = jnp.sum(err_share * err_share)
    feat_sum = jnp.sum(feats * maskg[:, None], axis=0)
    local_loss = square_sum + sparsity_weight * jnp.sum(feat_sum * norm_sum)
    dfeat = 2.0 * lax.dot_general(
        err16, w_dec, (((1,), (1,)), ((), ())), preferred_element_type=jnp.float32
    )
    dfeat = dfeat + sparsity_weight * maskg[:, None] * norm_sum[None, :]
    dpre16 = (dfeat * 2.0 * act).astype(jnp.bfloat16)
    enc_term = lax.dot_general(
        xg, dpre16, (((0,), (0,)), ((), ())), preferred_element_type=jnp.float32
    )
    enc_term = enc_term.reshape(2, half, local_latents)
    dec_term = 2.0 * lax.dot_general(
        feats16, err16, (((0,), (0,)), ((), ())), preferred_element_type=jnp.float32
    )
    scale = jnp.where(
        column_ids[None, :] < half, (feat_sum / norm_base)[:, None], (feat_sum / norm_inst)[:, None]
    )
    dec_term = dec_term + sparsity_weight * scale * w_dec.astype(jnp.float32)
    enc_total = lax.psum_scatter(
        enc_term.astype(jnp.bfloat16), "dp", scatter_dimension=1, tiled=True
    ).astype(jnp.float32)
    dec_total = lax.psum_scatter(
        dec_term.astype(jnp.bfloat16), "dp", scatter_dimension=1, tiled=True
    ).astype(jnp.float32)
    total, count = lax.psum((local_loss, own_count), ("dp", "latent"))
    factor = loss_scale / count
    grad_enc = (enc_total * factor).astype(jnp.bfloat16)
    grad_dec = (dec_total * factor).astype(jnp.bfloat16)
    loss = total / (count * width)
    return (grad_enc, grad_dec, loss)


def solution(mesh):
    return jax.shard_map(
        shards,
        mesh=mesh,
        in_specs=(
            P(("dp", "latent"), None),
            P(("dp", "latent")),
            P(("dp", "latent"), None),
            P(None, None, "latent"),
            P("latent"),
            P("latent", None),
            P(),
        ),
        out_specs=(P(None, "dp", "latent"), P("latent", "dp"), P()),
        check_vma=False,
    )
```

profile of v0, /device:TPU:1, one launch (start us, length us, event | category | flops | bytes accessed | tf_op | source)
XLA Modules:
  0.0 414.3 jit_solution(3964806186658669848)
XLA Ops:
  7.2 0.0 copy-start
  7.2 0.0 all-gather.3.cloned.1.call-start
  7.2 1.6 sort.17
  8.9 0.0 copy-done
  8.9 0.6 gather_fusion
  9.5 0.5 broadcast.57
  10.0 0.7 reduce.2
  10.7 0.1 reshape.95
  10.8 10.1 %all_to_all.14 = bf16[4,2,4096]{2,1,0:T(2,128)(2,1)S(1)} all-to-all(bf16[4,2,4096]{2,1,0:T(2,128)(2,1)S(1)} %reshape.95), channel_id=1, replica_groups=mesh['dp'=4,'latent'=32] {'dp'}, dimensions={0} | all-to-all | bytes 131072 | tf_op jit(solution)/shard_map/all_to_all | solution.py:25
  20.9 0.7 reshape.96
  21.6 0.0 all-gather.3.cloned.1.call-update
  22.3 0.6 gather_fusion.1
  23.0 0.6 fusion.25
  23.6 0.7 copy.17
  24.3 3.2 all-to-all-start.1
  27.5 0.0 all-reduce.4.cloned.1.call-start
  27.5 1.3 dynamic-slice
  29.6 1.9 all-to-all-done.1
  31.5 0.1 reduce.1
  31.6 0.2 dynamic-update-slice
  31.8 65.9 %all-reduce = bf16[128]{0:T(256)(128)(2,1)S(1)} all-reduce(bf16[128]{0:T(256)(128)(2,1)S(1)} %dynamic-update-slice), channel_id=2, replica_groups=mesh['dp'=4,'latent'=32] {'latent'}, use_global_device_ids=true, to_apply=%add | all-reduce | flops 128 | bytes 512
  97.7 0.0 all-gather.3.cloned.1.call-done
  97.8 7.3 %multiply_reduce_fusion = (f32[512]{0:T(512)S(1)}, f32[128,512]{1,0:T(8,128)S(1)}) fusion(f32[128]{0:T(128)S(1)} %mul.102, f32[512]{0:T(512)} %param.11, bf16[8192,512]{1,0:T(8,128)(2,1)} %bitcast.33, bf16[128,1,8192]{2,1,0:T(2,128)(2,1)} %all-gather.3.cloned.1.call-done), kind=kOutput, calls=%fused_computation.26 | convolution fusion | flops 1074068992 | bytes 10752512 | tf_op jit(solution)/shard_map/dot_general | solution.py:44
  105.1 6.0 %convolution_convert_fusion = bf16[128,8192]{1,0:T(8,128)(2,1)} fusion(bf16[512,8192]{1,0:T(8,128)(2,1)} %param.12, f32[128,512]{1,0:T(8,128)S(1)} %get-tuple-element.16), kind=kOutput, calls=%fused_computation.6 | convolution fusion | flops 1074921472 | bytes 10747904 | tf_op jit(solution)/shard_map/dot_general | solution.py:48
  111.0 0.0 all-reduce.4.cloned.1.call-update
  111.1 0.0 copy-start.2
  111.1 0.2 reduce-scatter.3.cloned.1.call-start
  111.3 11.3 %convert_multiply_fusion.1 = f32[512,8192]{1,0:T(8,128)} fusion(bf16[512,8192]{1,0:T(8,128)(2,1)} %param.12), kind=kLoop, calls=%fused_computation.3 | loop fusion | flops 8388608 | bytes 25165824 | tf_op jit(solution)/shard_map/square | solution.py:38
  122.6 0.0 copy-done.2
  122.6 6.5 %slice_reduce_fusion.1 = (f32[512]{0:T(512)S(1)}, f32[512]{0:T(512)S(1)}) fusion(f32[512,8192]{1,0:T(8,128)} %convert_multiply_fusion.1), kind=kLoop, calls=%fused_computation.8 | loop fusion | flops 4193280 | bytes 16781312 | tf_op jit(solution)/shard_map/reduce_sum | solution.py:39
  129.2 8.8 %copy.19 = bf16[128,1,8192]{0,2,1:T(8,128)(2,1)S(1)} copy(bf16[128,1,8192]{2,1,0:T(2,128)(2,1)} %all-gather.3.cloned.1.call-done) | data formatting | bytes 4194304 | tf_op jit(solution)/shard_map/dot_general | solution.py:61
  138.0 0.6 multiply_reduce_fusion.2
  138.6 75.9 %all-reduce.4.cloned.1.call-done = bf16[128,8192]{1,0:T(8,128)(2,1)} async-done(((bf16[128,8192]{1,0:T(8,128)(2,1)}), bf16[128,8192]{1,0:T(8,128)(2,1)}) %all-reduce.4.cloned.1.call-update) | async-done | bytes 2097168 | tf_op jit(solution)/shard_map/psum | solution.py:49
  214.5 8.7 %subtract_multiply_fusion = f32[128,8192]{1,0:T(8,128)} fusion(bf16[128,8192]{1,0:T(8,128)(2,1)} %all-reduce.4.cloned.1.call-done, f32[128]{0:T(128)S(1)} %mul.102, f32[8192]{0:T(1024)S(1)} %bitcast.36, bf16[128,1,8192]{2,1,0:T(2,128)(2,1)} %all-gather.3.cloned.1.call-done), kind=kLoop, calls=%fused_computation.12 | loop fusion | flops 5242880 | bytes 8421888 | tf_op jit(solution)/shard_map/mul | solution.py:50
  223.2 15.0 %convolution_convert_fusion.1 = bf16[2,4096,512]{2,1,0:T(8,128)(2,1)} fusion(bf16[2,4096,128]{2,1,0:T(8,128)(2,1)S(1)} %bitcast.34, f32[128,512]{1,0:T(8,128)S(1)} %get-tuple-element.16, bf16[512,8192]{1,0:T(8,128)(2,1)} %param.12, f32[128,8192]{1,0:T(8,128)} %subtract_multiply_fusion, f32[512]{0:T(512)S(1)} %get-tuple-element.10, f32[128]{0:T(128)S(1)} %mul.102), kind=kOutput, calls=%fused_computation.9 | convolution fusion | flops 2153119744 | bytes 23333376 | tf_op jit(solution)/shard_map/dot_general | solution.py:61
  238.2 0.0 reduce-scatter.3.cloned.1.call-update
  238.2 0.0 reduce-scatter.5.cloned.1.call-start
  238.3 9.8 %fusion.1 = bf16[512,8192]{1,0:T(8,128)(2,1)} fusion(bf16[512,8192]{1,0:T(8,128)(2,1)} %param.12, f32[512]{0:T(512)S(1)} %get-tuple-element.12, f32[512]{0:T(512)S(1)} %get-tuple-element.11, pred[8192]{0:T(1024)(128)(4,1)S(1)} %iota_compare_fusion, f32[128,8192]{1,0:T(8,128)} %subtract_multiply_fusion, f32[128,512]{1,0:T(8,128)S(1)} %get-tuple-element.16), kind=kOutput, calls=%fused_computation.5 | convolution fusion | flops 1100087296 | bytes 21245952 | tf_op jit(solution)/shard_map/dot_general | solution.py:65
  248.0 0.0 reduce-scatter.5.cloned.1.call-update
  248.1 1.6 multiply_reduce_fusion.1
  251.0 69.5 %all-reduce.1 = (f32[]{:T(128)}, f32[]{:T(128)}) all-reduce(f32[]{:T(128)} %get-tuple-element.13, f32[]{:T(128)S(6)} %add.86), channel_id=1, replica_groups=mesh['dp'=4,'latent'=32] {'dp','latent'}, use_global_device_ids=true, to_apply=%region_6.7 | all-reduce | flops 2 | bytes 16 | tf_op jit(solution)/shard_map/psum | solution.py:78
  321.8 0.0 copy-start.1
  322.5 0.0 reduce-scatter.3.cloned.1.call-done
  322.5 3.3 multiply_convert_fusion.1
  325.8 77.3 %reduce-scatter.5.cloned.1.call-done = bf16[512,2048]{1,0:T(8,128)(2,1)} async-done(((bf16[512,8192]{1,0:T(8,128)(2,1)}), bf16[512,2048]{1,0:T(8,128)(2,1)}) %reduce-scatter.5.cloned.1.call-update) | async-done | bytes 2097168 | tf_op jit(solution)/shard_map/reduce_scatter | solution.py:75
  403.2 3.4 multiply_convert_fusion
  406.6 0.0 copy-done.1
  (8 shorter events, 0.0 us)
Async XLA Ops:
  7.2 1.7 copy-start
  7.2 90.6 %all-gather.3.cloned.1.call-start = ((), (), s32[]{:S(2)}) async-start(), calls=%async_computation.4 | async-start | bytes 4325376 | tf_op jit(solution)/shard_map/all_gather | solution.py:29
  24.3 7.2 %all-to-all-start.1 = ((bf16[4,1,1]{2,1,0:T(2,128)(2,1)}), bf16[4,1,1]{2,1,0:T(2,128)(2,1)S(1)}, u32[]{:S(2)}, u32[]{:S(2)}) async-start(bf16[4,1,1]{2,1,0:T(2,128)(2,1)} %copy.17), calls=%async_computation.1 | async-start | bytes 4096 | tf_op jit(solution)/shard_map/all_to_all | solution.py:26
  27.5 187.0 %all-reduce.4.cloned.1.call-start = ((), (), s32[]{:S(2)}) async-start(), calls=%async_computation.5 | async-start | bytes 4194304 | tf_op jit(solution)/shard_map/psum | solution.py:49
  111.1 11.6 %copy-start.2 = (f32[2,4096]{1,0:T(2,128)S(1)}, f32[2,4096]{1,0:T(2,128)}, u32[]{:S(2)}) copy-start(f32[2,4096]{1,0:T(2,128)} %param.13) | copy-start | bytes 98308
  111.1 211.4 %reduce-scatter.3.cloned.1.call-start = ((), (), s32[]{:S(2)}) async-start(), calls=%async_computation.6 | async-start | bytes 10485760 | tf_op jit(solution)/shard_map/reduce_scatter | solution.py:72
  238.2 165.0 %reduce-scatter.5.cloned.1.call-start = ((), (), s32[]{:S(2)}) async-start(), calls=%async_computation.7 | async-start | bytes 10485760 | tf_op jit(solution)/shard_map/reduce_scatter | solution.py:75
  321.8 84.8 %copy-start.1 = (bf16[5,8192]{1,0:T(8,128)(2,1)S(1)}, bf16[5,8192]{1,0:T(8,128)(2,1)}, u32[]{:S(2)}) copy-start(bf16[5,8192]{1,0:T(8,128)(2,1)} %param.7) | copy-start | bytes 245764
Sparse Core Ops, SparseCore 0:
  21.8 47.3 all-gather.2
  111.2 103.2 all-reduce.3
  238.3 82.5 reduce-scatter.2
  323.2 79.8 reduce-scatter.4
where the time goes:
time: 415 us; the launch traced here: 414 us
  waiting for transfers between devices  155 us (37%)
  blocking collectives  145 us (35%)
  other arithmetic  38.6 us (9%)
  matrix products  38 us (9%)
  between operations  19.7 us (5%)
  local copies, waits for them, and re-layouts  13.6 us (3%)
    reduce_scatter x1, waiting for transfers between devices, shards(): lax.psum_scatter(dec_term.astype(jnp.bfloat16), 'dp', scatter_dimension=1...  77.3 us
    psum x1, waiting for transfers between devices, shards(): lax.psum(partial_value.astype(jnp.bfloat16), 'latent').astype(jnp.float32)  75.9 us
    psum x1, blocking collectives, shards(): total, count = lax.psum((local_loss, own_count), ('dp', 'latent'))  69.5 us
    unnamed x1, blocking collectives  65.9 us
    dot_general x1, matrix products, shards(): lax.dot_general(xg, dpre16, (((0,), (0,)), ((), ())), preferred_element_t...  15 us
    square x1, other arithmetic, shards(): squares_dec = jnp.square(w_dec.astype(jnp.float32))  11.3 us
    all_to_all x1, blocking collectives, shards(): lax.all_to_all(outgoing, 'dp', split_axis=0, concat_axis=0, tiled=True)  10.1 us
    dot_general x1, matrix products, shards(): lax.dot_general(feats16, err16, (((0,), (0,)), ((), ())), preferred_eleme...  9.77 us
  transfers between devices with their start and end apart: 5, of which 3 were waited for; matrix products, arithmetic and copies ran while one was open for 11% of the time, Pallas kernels for 0%

commit v1 on v0

--- a/solution.py
+++ b/solution.py
@@ -75,7 +75,7 @@
     dec_total = lax.psum_scatter(
         dec_term.astype(jnp.bfloat16), "dp", scatter_dimension=1, tiled=True
     ).astype(jnp.float32)
-    total, count = lax.psum((local_loss, own_count), ("dp", "latent"))
+    total, count = lax.psum(lax.psum((local_loss, own_count), "latent"), "dp")
     factor = loss_scale / count
     grad_enc = (enc_total * factor).astype(jnp.bfloat16)
     grad_dec = (dec_total * factor).astype(jnp.bfloat16)

time: 415 us -> 414 us (level)
    reduce_scatter x1, waiting for transfers between devices: 77.3 us -> 72.6 us  [shards(): lax.psum_scatter(dec_term.astype(jnp.bfloat16), 'dp', scatter_dimension=1...]
    psum x1 -> x2, blocking collectives: 69.5 us -> 72.7 us  [shards(): total, count = lax.psum(lax.psum((local_loss, own_count), 'latent'), 'dp')]
where the time goes in v1:
time: 414 us; the launch traced here: 413 us
  waiting for transfers between devices  151 us (36%)
  blocking collectives  149 us (36%)
  other arithmetic  38.6 us (9%)
  matrix products  38 us (9%)
  between operations  19.7 us (5%)
  local copies, waits for them, and re-layouts  13.6 us (3%)
    psum x1, waiting for transfers between devices, shards(): lax.psum(partial_value.astype(jnp.bfloat16), 'latent').astype(jnp.float32)  75.9 us
    psum x2, blocking collectives, shards(): total, count = lax.psum(lax.psum((local_loss, own_count), 'latent'), 'dp')  72.7 us
    reduce_scatter x1, waiting for transfers between devices, shards(): lax.psum_scatter(dec_term.astype(jnp.bfloat16), 'dp', scatter_dimension=1...  72.6 us
    unnamed x1, blocking collectives  65.9 us
    dot_general x1, matrix products, shards(): lax.dot_general(xg, dpre16, (((0,), (0,)), ((), ())), preferred_element_t...  15 us
    square x1, other arithmetic, shards(): squares_dec = jnp.square(w_dec.astype(jnp.float32))  11.3 us
    all_to_all x1, blocking collectives, shards(): lax.all_to_all(outgoing, 'dp', split_axis=0, concat_axis=0, tiled=True)  10.1 us
    dot_general x1, matrix products, shards(): lax.dot_general(feats16, err16, (((0,), (0,)), ((), ())), preferred_eleme...  9.77 us
  transfers between devices with their start and end apart: 5, of which 3 were waited for; matrix products, arithmetic and copies ran while one was open for 11% of the time, Pallas kernels for 0%

profile of v1, /device:TPU:1, one launch (start us, length us, event | category | flops | bytes accessed | tf_op | source)
XLA Modules:
  0.0 412.8 jit_solution(11487368720616788245)
XLA Ops:
  7.2 0.0 copy-start
  7.2 0.0 all-gather.3.cloned.1.call-start
  7.2 1.6 sort.17
  8.9 0.0 copy-done
  8.9 0.6 gather_fusion
  9.5 0.5 broadcast.57
  10.0 0.7 reduce.2
  10.7 0.1 reshape.95
  10.8 10.1 %all_to_all.14 = bf16[4,2,4096]{2,1,0:T(2,128)(2,1)S(1)} all-to-all(bf16[4,2,4096]{2,1,0:T(2,128)(2,1)S(1)} %reshape.95), channel_id=1, replica_groups=mesh['dp'=4,'latent'=32] {'dp'}, dimensions={0} | all-to-all | bytes 131072 | tf_op jit(solution)/shard_map/all_to_all | solution.py:25
  20.9 0.7 reshape.96
  21.6 0.0 all-gather.3.cloned.1.call-update
  22.3 0.6 gather_fusion.1
  23.0 0.6 fusion.25
  23.6 0.7 copy.17
  24.3 3.2 all-to-all-start.1
  27.5 0.0 all-reduce.5.cloned.1.call-start
  27.5 1.3 dynamic-slice
  29.6 1.9 all-to-all-done.1
  31.5 0.1 reduce.1
  31.6 0.2 dynamic-update-slice
  31.8 65.9 %all-reduce = bf16[128]{0:T(256)(128)(2,1)S(1)} all-reduce(bf16[128]{0:T(256)(128)(2,1)S(1)} %dynamic-update-slice), channel_id=2, replica_groups=mesh['dp'=4,'latent'=32] {'latent'}, use_global_device_ids=true, to_apply=%add | all-reduce | flops 128 | bytes 512
  97.7 0.0 all-gather.3.cloned.1.call-done
  97.8 7.3 %multiply_reduce_fusion = (f32[512]{0:T(512)S(1)}, f32[128,512]{1,0:T(8,128)S(1)}) fusion(f32[128]{0:T(128)S(1)} %mul.102, f32[512]{0:T(512)} %param.11, bf16[8192,512]{1,0:T(8,128)(2,1)} %bitcast.33, bf16[128,1,8192]{2,1,0:T(2,128)(2,1)} %all-gather.3.cloned.1.call-done), kind=kOutput, calls=%fused_computation.26 | convolution fusion | flops 1074068992 | bytes 10752512 | tf_op jit(solution)/shard_map/dot_general | solution.py:44
  105.1 6.0 %convolution_convert_fusion = bf16[128,8192]{1,0:T(8,128)(2,1)} fusion(bf16[512,8192]{1,0:T(8,128)(2,1)} %param.12, f32[128,512]{1,0:T(8,128)S(1)} %get-tuple-element.18), kind=kOutput, calls=%fused_computation.6 | convolution fusion | flops 1074921472 | bytes 10747904 | tf_op jit(solution)/shard_map/dot_general | solution.py:48
  111.0 0.0 all-reduce.5.cloned.1.call-update
  111.1 0.0 copy-start.2
  111.1 0.2 reduce-scatter.3.cloned.1.call-start
  111.3 11.3 %convert_multiply_fusion.1 = f32[512,8192]{1,0:T(8,128)} fusion(bf16[512,8192]{1,0:T(8,128)(2,1)} %param.12), kind=kLoop, calls=%fused_computation.3 | loop fusion | flops 8388608 | bytes 25165824 | tf_op jit(solution)/shard_map/square | solution.py:38
  122.6 0.0 copy-done.2
  122.6 6.5 %slice_reduce_fusion.1 = (f32[512]{0:T(512)S(1)}, f32[512]{0:T(512)S(1)}) fusion(f32[512,8192]{1,0:T(8,128)} %convert_multiply_fusion.1), kind=kLoop, calls=%fused_computation.8 | loop fusion | flops 4193280 | bytes 16781312 | tf_op jit(solution)/shard_map/reduce_sum | solution.py:39
  129.2 8.8 %copy.19 = bf16[128,1,8192]{0,2,1:T(8,128)(2,1)S(1)} copy(bf16[128,1,8192]{2,1,0:T(2,128)(2,1)} %all-gather.3.cloned.1.call-done) | data formatting | bytes 4194304 | tf_op jit(solution)/shard_map/dot_general | solution.py:61
  138.0 0.6 multiply_reduce_fusion.2
  138.6 75.9 %all-reduce.5.cloned.1.call-done = bf16[128,8192]{1,0:T(8,128)(2,1)} async-done(((bf16[128,8192]{1,0:T(8,128)(2,1)}), bf16[128,8192]{1,0:T(8,128)(2,1)}) %all-reduce.5.cloned.1.call-update) | async-done | bytes 2097168 | tf_op jit(solution)/shard_map/psum | solution.py:49
  214.5 8.7 %subtract_multiply_fusion = f32[128,8192]{1,0:T(8,128)} fusion(bf16[128,8192]{1,0:T(8,128)(2,1)} %all-reduce.5.cloned.1.call-done, f32[128]{0:T(128)S(1)} %mul.102, f32[8192]{0:T(1024)S(1)} %bitcast.36, bf16[128,1,8192]{2,1,0:T(2,128)(2,1)} %all-gather.3.cloned.1.call-done), kind=kLoop, calls=%fused_computation.12 | loop fusion | flops 5242880 | bytes 8421888 | tf_op jit(solution)/shard_map/mul | solution.py:50
  223.2 15.0 %convolution_convert_fusion.1 = bf16[2,4096,512]{2,1,0:T(8,128)(2,1)} fusion(bf16[2,4096,128]{2,1,0:T(8,128)(2,1)S(1)} %bitcast.34, f32[128,512]{1,0:T(8,128)S(1)} %get-tuple-element.18, bf16[512,8192]{1,0:T(8,128)(2,1)} %param.12, f32[128,8192]{1,0:T(8,128)} %subtract_multiply_fusion, f32[512]{0:T(512)S(1)} %get-tuple-element.12, f32[128]{0:T(128)S(1)} %mul.102), kind=kOutput, calls=%fused_computation.9 | convolution fusion | flops 2153119744 | bytes 23333376 | tf_op jit(solution)/shard_map/dot_general | solution.py:61
  238.2 0.0 reduce-scatter.3.cloned.1.call-update
  238.2 0.0 reduce-scatter.5.cloned.1.call-start
  238.3 9.8 %fusion.1 = bf16[512,8192]{1,0:T(8,128)(2,1)} fusion(bf16[512,8192]{1,0:T(8,128)(2,1)} %param.12, f32[512]{0:T(512)S(1)} %get-tuple-element.14, f32[512]{0:T(512)S(1)} %get-tuple-element.13, pred[8192]{0:T(1024)(128)(4,1)S(1)} %iota_compare_fusion, f32[128,8192]{1,0:T(8,128)} %subtract_multiply_fusion, f32[128,512]{1,0:T(8,128)S(1)} %get-tuple-element.18), kind=kOutput, calls=%fused_computation.5 | convolution fusion | flops 1100087296 | bytes 21245952 | tf_op jit(solution)/shard_map/dot_general | solution.py:65
  248.0 0.0 reduce-scatter.5.cloned.1.call-update
  248.1 1.6 multiply_reduce_fusion.1
  251.0 63.5 %all-reduce.1 = (f32[]{:T(128)}, f32[]{:T(128)}) all-reduce(f32[]{:T(128)} %get-tuple-element.15, f32[]{:T(128)S(6)} %add.90), channel_id=1, replica_groups=mesh['dp'=4,'latent'=32] {'latent'}, use_global_device_ids=true, to_apply=%region_6.7 | all-reduce | flops 2 | bytes 16 | tf_op jit(solution)/shard_map/psum | solution.py:78
  314.4 9.3 %all-reduce.2 = (f32[]{:T(128)}, f32[]{:T(128)}) all-reduce(f32[]{:T(128)} %get-tuple-element.7, f32[]{:T(128)} %get-tuple-element.8), channel_id=1, replica_groups=mesh['dp'=4,'latent'=32] {'dp'}, use_global_device_ids=true, to_apply=%region_7.8 | all-reduce | flops 2 | bytes 16 | tf_op jit(solution)/shard_map/psum | solution.py:78
  325.1 0.0 copy-start.1
  325.8 0.0 reduce-scatter.3.cloned.1.call-done
  325.8 3.3 multiply_convert_fusion.1
  329.1 72.6 %reduce-scatter.5.cloned.1.call-done = bf16[512,2048]{1,0:T(8,128)(2,1)} async-done(((bf16[512,8192]{1,0:T(8,128)(2,1)}), bf16[512,2048]{1,0:T(8,128)(2,1)}) %reduce-scatter.5.cloned.1.call-update) | async-done | bytes 2097168 | tf_op jit(solution)/shard_map/reduce_scatter | solution.py:75
  401.7 3.4 multiply_convert_fusion
  405.1 0.0 copy-done.1
  (8 shorter events, 0.0 us)
Async XLA Ops:
  7.2 1.7 copy-start
  7.2 90.6 %all-gather.3.cloned.1.call-start = ((), (), s32[]{:S(2)}) async-start(), calls=%async_computation.4 | async-start | bytes 4325376 | tf_op jit(solution)/shard_map/all_gather | solution.py:29
  24.3 7.2 %all-to-all-start.1 = ((bf16[4,1,1]{2,1,0:T(2,128)(2,1)}), bf16[4,1,1]{2,1,0:T(2,128)(2,1)S(1)}, u32[]{:S(2)}, u32[]{:S(2)}) async-start(bf16[4,1,1]{2,1,0:T(2,128)(2,1)} %copy.17), calls=%async_computation.1 | async-start | bytes 4096 | tf_op jit(solution)/shard_map/all_to_all | solution.py:26
  27.5 187.0 %all-reduce.5.cloned.1.call-start = ((), (), s32[]{:S(2)}) async-start(), calls=%async_computation.5 | async-start | bytes 4194304 | tf_op jit(solution)/shard_map/psum | solution.py:49
  111.1 11.6 %copy-start.2 = (f32[2,4096]{1,0:T(2,128)S(1)}, f32[2,4096]{1,0:T(2,128)}, u32[]{:S(2)}) copy-start(f32[2,4096]{1,0:T(2,128)} %param.13) | copy-start | bytes 98308
  111.1 214.7 %reduce-scatter.3.cloned.1.call-start = ((), (), s32[]{:S(2)}) async-start(), calls=%async_computation.6 | async-start | bytes 10485760 | tf_op jit(solution)/shard_map/reduce_scatter | solution.py:72
  238.2 163.5 %reduce-scatter.5.cloned.1.call-start = ((), (), s32[]{:S(2)}) async-start(), calls=%async_computation.7 | async-start | bytes 10485760 | tf_op jit(solution)/shard_map/reduce_scatter | solution.py:75
  325.1 80.1 %copy-start.1 = (bf16[5,8192]{1,0:T(8,128)(2,1)S(1)}, bf16[5,8192]{1,0:T(8,128)(2,1)}, u32[]{:S(2)}) copy-start(bf16[5,8192]{1,0:T(8,128)(2,1)} %param.7) | copy-start | bytes 245764
Sparse Core Ops, SparseCore 0:
  21.8 47.3 all-gather.2
  111.2 103.2 all-reduce.4
  238.3 80.6 reduce-scatter.2
  321.3 80.3 reduce-scatter.4
